TPU v7x, 32 devices: a whole 2x2x4 slice. The times are simulated.
32 devices in a mesh: atlas: 4 (over y, x), row: 2 (over core), col: 4 (over z).
Axes of the slice: x: 2, y: 2, z: 4, core: 2. Of those that a mesh axis runs over, the one named last changes fastest.
Arguments:
- cells: bfloat16 [4, 64, 1024], P('atlas', None, 'row'), may hold values from -4 to 4
- support: bfloat16 [64, 16384], P(None, 'col'), may hold values from -4 to 4
Outputs:
- cell_dual: float32 [4, 1024], P('atlas', 'row')
- support_dual: float32 [4, 16384], P('atlas', 'col')
- new_support: float32 [64, 16384], P(None, 'col')
All inputs are finite; a program needn't handle non-finite values.
Results may differ from a plain program's by a relative error of at most 0.001.
Values sent between devices are 32-bit elements; how exact they have to be, the bound alone decides.
No kernel may reach another device: no remote copies, remote signals or barrier semaphores. Data moves between devices by JAX's collectives and lax.ppermute only.
A program may use at most 64 MiB of HBM per device.

v0:
```python
import jax
import jax.numpy as jnp
from jax import lax
from jax.sharding import PartitionSpec as P

ITERS = 2
blur = 0.1


def combined_all(value, axis, join):
    pieces = jax.tree.map(lambda part: lax.all_gather(part, axis), value)
    head = jax.tree.map(lambda part: part[0], pieces)
    tail = jax.tree.map(lambda part: part[1:], pieces)
    subtotal, _ = lax.scan(lambda subtotal, slab: (join(subtotal, slab), None), head, tail)
    return subtotal


def lse_pair(first, second):
    top_one, total_one = first
    top_two, total_two = second
    peak = jnp.maximum(top_one, top_two)
    return (peak, total_one * jnp.exp(top_one - peak) + total_two * jnp.exp(top_two - peak))


def shards(cells, support):
    points = cells[0]
    dims, rows = points.shape
    columns = support.shape[1]
    width_block = min(512, columns)
    count = columns // width_block
    points_wide = points.astype(jnp.float32)
    squares_x = jnp.sum(jnp.square(points_wide), axis=0)
    squares_y = jnp.sum(jnp.square(support.astype(jnp.float32)), axis=0)
    total_cells = rows * lax.axis_size("row")
    total_support = columns * lax.axis_size("col")
    atlases = lax.axis_size("atlas")

    def tile_cost(start):
        piece = lax.dynamic_slice_in_dim(support, start, width_block, 1)
        near = lax.dynamic_slice_in_dim(squares_y, start, width_block, 0)
        cross = lax.dot_general(
            points, piece, (((0,), (0,)), ((), ())), preferred_element_type=jnp.float32
        )
        return (squares_x[:, None] + near[None, :] - 2.0 * cross) / dims

    def row_step(dual_g):

        def row_visit(index, carry):
            top, total = carry
            start = index * width_block
            gpart = lax.dynamic_slice_in_dim(dual_g, start, width_block, 0)
            logits = (gpart[None, :] - tile_cost(start)) / blur
            peak = jnp.maximum(top, jnp.max(logits, axis=1))
            total = total * jnp.exp(top - peak) + jnp.sum(jnp.exp(logits - peak[:, None]), axis=1)
            return (peak, total)

        start_carry = (jnp.full((rows,), -jnp.inf, jnp.float32), jnp.zeros((rows,), jnp.float32))
        top, total = lax.fori_loop(0, count, row_visit, start_carry)
        top, total = combined_all((top, total), "col", lse_pair)
        return blur * jnp.log(1.0 / total_cells) - blur * (top + jnp.log(total))

    def column_step(dual_f):

        def column_visit(index, carry):
            top, total = carry
            start = index * width_block
            logits = (dual_f[:, None] - tile_cost(start)) / blur
            peak = jnp.max(logits, axis=0)
            mass = jnp.sum(jnp.exp(logits - peak[None, :]), axis=0)
            return (
                lax.dynamic_update_slice_in_dim(top, peak, start, 0),
                lax.dynamic_update_slice_in_dim(total, mass, start, 0),
            )

        start_carry = (jnp.zeros((columns,), jnp.float32), jnp.zeros((columns,), jnp.float32))
        top, total = lax.fori_loop(0, count, column_visit, start_carry)
        top, total = combined_all((top, total), "row", lse_pair)
        return blur * jnp.log(1.0 / total_support) - blur * (top + jnp.log(total))

    dual_g = jnp.zeros((columns,), jnp.float32)
    dual_f = jnp.zeros((rows,), jnp.float32)
    for step in range(ITERS):
        dual_f = row_step(dual_g)
        dual_g = column_step(dual_f)

    def positions_visit(index, summed):
        start = index * width_block
        gpart = lax.dynamic_slice_in_dim(dual_g, start, width_block, 0)
        plan = jnp.exp((dual_f[:, None] + gpart[None, :] - tile_cost(start)) / blur)
        moved = jnp.dot(points_wide, plan, precision=lax.Precision.HIGHEST) * total_support
        return lax.dynamic_update_slice_in_dim(summed, moved, start, 1)

    terms = lax.fori_loop(0, count, positions_visit, jnp.zeros((dims, columns), jnp.float32))
    summed = lax.psum(terms, ("atlas", "row"))
    updated = summed / atlases
    return (dual_f[None, :], dual_g[None, :], updated)


def solution(mesh):
    in_specs = (P("atlas", None, "row"), P(None, "col"))
    out_specs = (P("atlas", "row"), P("atlas", "col"), P(None, "col"))
    return jax.shard_map(shards, mesh=mesh, in_specs=in_specs, out_specs=out_specs, check_vma=False)
```

profile of v0, /device:TPU:0, one launch (start us, length us, event | category | flops | bytes accessed | tf_op | source)
XLA Modules:
  0.0 182.5 jit_solution(9270883459431666822)
XLA Ops:
  7.3 0.9 multiply_reduce_fusion.1
  8.2 1.2 multiply_reduce_fusion
  9.4 6.2 %while.114 = (s32[]{:T(128)}, f32[512]{0:T(512)S(1)}, f32[512]{0:T(512)S(1)}, f32[512]{0:T(512)S(1)}, f32[4096]{0:T(1024)S(1)}, /*index=5*/bf16[64,4096]{1,0:T(8...) while((s32[]{:T(128)}, f32[512]{0:T(512)S(1)}, ...), condition=%wide.region_5.0_spmd.clone, body=%wide.region_2.0_spmd.clone.sunk | while | flops 35916292 | bytes 2263222 | solution.py:58
  15.6 13.6 %all-gather.8 = f32[4,1,512]{2,1,0:T(1,128)S(1)} all-gather(f32[1,1,512]{2,1,0:T(1,128)S(1)} %bitcast.124), channel_id=2, replica_groups=mesh['atlas'=4,'row'=2,'col'=4] {'col'}, dimensions={0}, use_global_device_ids=true | all-gather | bytes 10240 | tf_op jit(solution)/shard_map/all_gather | solution.py:11
  29.3 0.6 copy-done.4
  29.9 11.9 %all-gather.9 = f32[4,1,512]{2,1,0:T(1,128)S(1)} all-gather(f32[1,1,512]{2,1,0:T(1,128)S(1)} %bitcast.134), channel_id=3, replica_groups=mesh['atlas'=4,'row'=2,'col'=4] {'col'}, dimensions={0}, use_global_device_ids=true | all-gather | bytes 10240 | tf_op jit(solution)/shard_map/all_gather | solution.py:11
  41.8 0.7 slice-done.3
  42.5 0.7 slice-done.2
  43.4 10.0 %while.110 = (s32[]{:T(128)}, f32[4096]{0:T(1024)S(1)}, f32[4096]{0:T(1024)S(1)}, f32[512]{0:T(512)S(1)}, f32[512]{0:T(512)S(1)}, /*index=5*/f32[4096]{0:T(1024)...) while((s32[]{:T(128)}, f32[4096]{0:T(1024)S(1)}, ...), condition=%wide.region_11.12_spmd, body=%wide.region_8.11_spmd.sunk | while | flops 35912708 | bytes 2252979 | solution.py:76
  44.7 0.5 fusion.78
  47.3 0.5 fusion.78
  49.8 0.5 fusion.78
  52.2 0.5 fusion.78
  53.4 1.8 all-gather.3
  55.2 1.8 all-gather.2
  57.0 6.8 %while.115 = (s32[]{:T(128)}, f32[512]{0:T(512)S(1)}, f32[512]{0:T(512)S(1)}, f32[4096]{0:T(1024)S(1)}, f32[512]{0:T(512)S(1)}, /*index=5*/f32[4096]{0:T(1024)S(...) while((s32[]{:T(128)}, f32[512]{0:T(512)S(1)}, ...), condition=%wide.region_15.16_spmd.clone, body=%wide.region_12.0_spmd.clone.sunk | while | flops 35916292 | bytes 2269378 | solution.py:58
  63.9 11.9 %all-gather.10 = f32[4,1,512]{2,1,0:T(1,128)S(1)} all-gather(f32[1,1,512]{2,1,0:T(1,128)S(1)} %bitcast.123), channel_id=6, replica_groups=mesh['atlas'=4,'row'=2,'col'=4] {'col'}, dimensions={0}, use_global_device_ids=true | all-gather | bytes 10240 | tf_op jit(solution)/shard_map/all_gather | solution.py:11
  75.8 0.6 copy-done.3
  76.4 11.9 %all-gather.11 = f32[4,1,512]{2,1,0:T(1,128)S(1)} all-gather(f32[1,1,512]{2,1,0:T(1,128)S(1)} %bitcast.133), channel_id=7, replica_groups=mesh['atlas'=4,'row'=2,'col'=4] {'col'}, dimensions={0}, use_global_device_ids=true | all-gather | bytes 10240 | tf_op jit(solution)/shard_map/all_gather | solution.py:11
  88.3 0.6 copy-done.5
  88.9 0.7 slice-done.1
  89.6 0.7 slice-done.5
  90.3 0.7 slice-done.4
  91.2 10.0 %while.112 = (s32[]{:T(128)}, f32[4096]{0:T(1024)S(1)}, f32[4096]{0:T(1024)S(1)}, f32[512]{0:T(512)S(1)}, f32[512]{0:T(512)S(1)}, /*index=5*/f32[4096]{0:T(1024)...) while((s32[]{:T(128)}, f32[4096]{0:T(1024)S(1)}, ...), condition=%wide.region_21.22_spmd, body=%wide.region_18.0_spmd.sunk | while | flops 35912708 | bytes 2252979 | solution.py:76
  100.1 0.5 fusion.80
  101.2 1.8 all-gather.7
  103.0 1.8 all-gather.6
  104.9 12.0 %while.113 = (s32[]{:T(128)}, f32[64,4096]{1,0:T(8,128)S(1)}, f32[512]{0:T(512)S(1)}, f32[4096]{0:T(1024)S(1)}, f32[512]{0:T(512)S(1)}, /*index=5*/f32[4096]{0:T...) while((s32[]{:T(128)}, f32[64,4096]{1,0:T(8,128)S(1)}, ...), condition=%wide.region_23.24_spmd, body=%wide.region_22.23_spmd.sunk | while | flops 236748800 | bytes 2506939 | solution.py:93
  105.1 0.5 fusion.85
  105.6 0.8 fusion.86
  106.6 0.5 fusion.85
  107.1 0.8 fusion.86
  108.1 0.5 fusion.85
  108.6 0.8 fusion.86
  109.6 0.5 fusion.85
  110.1 0.8 fusion.86
  111.1 0.5 fusion.85
  111.6 0.8 fusion.86
  112.6 0.5 fusion.85
  113.1 0.8 fusion.86
  114.1 0.5 fusion.85
  114.6 0.8 fusion.86
  115.6 0.5 fusion.85
  116.1 0.8 fusion.86
  116.9 0.6 copy-done.6
  117.9 0.7 multiply_subtract_fusion.1
  118.6 54.8 %all-reduce.2.cloned.1.call-done = f32[64,4096]{1,0:T(8,128)} async-done(((f32[64,4096]{1,0:T(8,128)}), f32[64,4096]{1,0:T(8,128)}) %all-reduce.2.cloned.1.call-update) | async-done | bytes 1048592 | tf_op jit(solution)/shard_map/psum | solution.py:94
  173.4 2.3 %broadcast_multiply_fusion = f32[64,4096]{1,0:T(8,128)} fusion(f32[64,4096]{1,0:T(8,128)} %all-reduce.2.cloned.1.call-done), kind=kLoop, calls=%fused_computation.61 | loop fusion | flops 262144 | bytes 2097152 | tf_op jit(solution)/shard_map/div | solution.py:95
  (248 shorter events, 32.5 us)
Async XLA Ops:
  7.2 2.2 %copy-start.1 = (bf16[64,4096]{1,0:T(8,128)(2,1)S(1)}, bf16[64,4096]{1,0:T(8,128)(2,1)}, u32[]{:S(2)}) copy-start(bf16[64,4096]{1,0:T(8,128)(2,1)} %param.17) | copy-start | bytes 1572868
  7.2 166.2 %all-reduce.2.cloned.1.call-start = ((), (), s32[]{:S(2)}) async-start(), calls=%async_computation | async-start | bytes 2097152 | tf_op jit(solution)/shard_map/psum | solution.py:94
  8.2 1.2 copy-start.2
  29.3 0.6 copy-start.4
  41.8 0.7 slice-start.3
  42.5 0.7 slice-start.2
  75.8 0.6 copy-start.3
  88.3 0.6 copy-start.5
  88.9 0.7 slice-start.1
  89.6 0.7 slice-start.5
  90.3 0.7 slice-start.4
  90.3 0.7 slice-start
  116.9 0.6 copy-start.6
  116.9 1.0 copy-start
Sparse Core Ops, SparseCore 0:
  118.0 55.2 all-reduce.1
where the time goes:
time: 183 us; the launch traced here: 182 us
  blocking collectives  56.7 us (31%)
  waiting for transfers between devices  54.8 us (30%)
  matrix products  25.1 us (14%)
  local copies, waits for them, and re-layouts  18.8 us (10%)
  between operations  14.2 us (8%)
  other arithmetic  12 us (7%)
    all_gather x8, blocking collectives, combined_all(): pieces = jax.tree.map(lambda part: lax.all_gather(part, axis), value)  56.7 us
    psum x1, waiting for transfers between devices, shards(): summed = lax.psum(terms, ('atlas', 'row'))  54.8 us
    dot_general x40, matrix products, tile_cost(): lax.dot_general(points, piece, (((0,), (0,)), ((), ())), preferred_elemen...  18.7 us
    dot_general x8, matrix products, positions_visit(): jnp.dot(points_wide, plan, precision=lax.Precision.HIGHEST) * total_support  6.37 us
    dynamic_update_slice x16, local copies, waits for them, and re-layouts, column_visit(): lax.dynamic_update_slice_in_dim(top, peak, start, 0)  4.3 us
    dynamic_update_slice x16, local copies, waits for them, and re-layouts, column_visit(): lax.dynamic_update_slice_in_dim(total, mass, start, 0)  3.85 us
  transfers between devices with their start and end apart: 1, of which 1 were waited for; matrix products, arithmetic and copies ran while one was open for 0% of the time, Pallas kernels for 0%

commit v1 on v0

--- a/solution.py
+++ b/solution.py
@@ -91,7 +91,8 @@
         return lax.dynamic_update_slice_in_dim(summed, moved, start, 1)
 
     terms = lax.fori_loop(0, count, positions_visit, jnp.zeros((dims, columns), jnp.float32))
-    summed = lax.psum(terms, ("atlas", "row"))
+    convert_trails = lambda incoming_x: lax.psum(lax.psum(incoming_x, "row"), "atlas")
+    summed = convert_trails(terms)
     updated = summed / atlases
     return (dual_f[None, :], dual_g[None, :], updated)
 

time: 183 us -> 202 us (1.10)
  waiting for transfers between devices: 54.8 us -> 74.2 us
    psum x1 -> x2, waiting for transfers between devices: 54.8 us -> 74.2 us  [the longest x1 56 us: shards(): lax.psum(lax.psum(incoming_x, 'row'), 'atlas')]
  transfers between devices with their start and end apart: 1 -> 2, of which waited for: 1 -> 2; matrix products, arithmetic and copies ran while one was open for 0% -> 0% of each run, Pallas kernels for 0% -> 0%
where the time goes in v1:
time: 202 us
  waiting for transfers between devices  74.2 us (37%)
  blocking collectives  56.7 us (28%)
  matrix products  25.1 us (12%)
  local copies, waits for them, and re-layouts  18.8 us (9%)
  between operations  14.2 us (7%)
  other arithmetic  12 us (6%)
    all_gather x8, blocking collectives, combined_all(): pieces = jax.tree.map(lambda part: lax.all_gather(part, axis), value)  56.7 us
    psum x1, waiting for transfers between devices, shards(): lax.psum(lax.psum(incoming_x, 'row'), 'atlas')  56 us
    dot_general x40, matrix products, tile_cost(): lax.dot_general(points, piece, (((0,), (0,)), ((), ())), preferred_elemen...  18.7 us
    psum x1, waiting for transfers between devices, shards(): lax.psum(incoming_x, 'row')  18.1 us
    dot_general x8, matrix products, positions_visit(): jnp.dot(points_wide, plan, precision=lax.Precision.HIGHEST) * total_support  6.37 us
    dynamic_update_slice x16, local copies, waits for them, and re-layouts, column_visit(): lax.dynamic_update_slice_in_dim(top, peak, start, 0)  4.3 us
  transfers between devices with their start and end apart: 2, of which 2 were waited for; matrix products, arithmetic and copies ran while one was open for 0% of the time, Pallas kernels for 0%

profile of v1, /device:TPU:0, one launch (start us, length us, event | category | flops | bytes accessed | tf_op | source)
XLA Modules:
  0.0 201.9 jit_solution(5671251769491468852)
XLA Ops:
  7.3 0.9 multiply_reduce_fusion.1
  8.2 1.2 multiply_reduce_fusion
  9.4 6.2 %while.114 = (s32[]{:T(128)}, f32[512]{0:T(512)S(1)}, f32[512]{0:T(512)S(1)}, f32[512]{0:T(512)S(1)}, f32[4096]{0:T(1024)S(1)}, /*index=5*/bf16[64,4096]{1,0:T(8...) while((s32[]{:T(128)}, f32[512]{0:T(512)S(1)}, ...), condition=%wide.region_5.0_spmd.clone, body=%wide.region_2.0_spmd.clone.sunk | while | flops 35916292 | bytes 2263222 | solution.py:58
  15.6 13.6 %all-gather.8 = f32[4,1,512]{2,1,0:T(1,128)S(1)} all-gather(f32[1,1,512]{2,1,0:T(1,128)S(1)} %bitcast.124), channel_id=2, replica_groups=mesh['atlas'=4,'row'=2,'col'=4] {'col'}, dimensions={0}, use_global_device_ids=true | all-gather | bytes 10240 | tf_op jit(solution)/shard_map/all_gather | solution.py:11
  29.3 0.6 copy-done.4
  29.9 11.9 %all-gather.9 = f32[4,1,512]{2,1,0:T(1,128)S(1)} all-gather(f32[1,1,512]{2,1,0:T(1,128)S(1)} %bitcast.134), channel_id=3, replica_groups=mesh['atlas'=4,'row'=2,'col'=4] {'col'}, dimensions={0}, use_global_device_ids=true | all-gather | bytes 10240 | tf_op jit(solution)/shard_map/all_gather | solution.py:11
  41.8 0.7 slice-done.3
  42.5 0.7 slice-done.2
  43.4 10.0 %while.110 = (s32[]{:T(128)}, f32[4096]{0:T(1024)S(1)}, f32[4096]{0:T(1024)S(1)}, f32[512]{0:T(512)S(1)}, f32[512]{0:T(512)S(1)}, /*index=5*/f32[4096]{0:T(1024)...) while((s32[]{:T(128)}, f32[4096]{0:T(1024)S(1)}, ...), condition=%wide.region_11.12_spmd, body=%wide.region_8.11_spmd.sunk | while | flops 35912708 | bytes 2252979 | solution.py:76
  47.3 0.5 fusion.78
  49.8 0.5 fusion.78
  52.2 0.5 fusion.78
  53.4 1.8 all-gather.3
  55.2 1.8 all-gather.2
  57.0 6.8 %while.115 = (s32[]{:T(128)}, f32[512]{0:T(512)S(1)}, f32[512]{0:T(512)S(1)}, f32[4096]{0:T(1024)S(1)}, f32[512]{0:T(512)S(1)}, /*index=5*/f32[4096]{0:T(1024)S(...) while((s32[]{:T(128)}, f32[512]{0:T(512)S(1)}, ...), condition=%wide.region_15.16_spmd.clone, body=%wide.region_12.0_spmd.clone.sunk | while | flops 35916292 | bytes 2269378 | solution.py:58
  63.9 11.9 %all-gather.10 = f32[4,1,512]{2,1,0:T(1,128)S(1)} all-gather(f32[1,1,512]{2,1,0:T(1,128)S(1)} %bitcast.123), channel_id=6, replica_groups=mesh['atlas'=4,'row'=2,'col'=4] {'col'}, dimensions={0}, use_global_device_ids=true | all-gather | bytes 10240 | tf_op jit(solution)/shard_map/all_gather | solution.py:11
  75.8 0.6 copy-done.3
  76.4 11.9 %all-gather.11 = f32[4,1,512]{2,1,0:T(1,128)S(1)} all-gather(f32[1,1,512]{2,1,0:T(1,128)S(1)} %bitcast.133), channel_id=7, replica_groups=mesh['atlas'=4,'row'=2,'col'=4] {'col'}, dimensions={0}, use_global_device_ids=true | all-gather | bytes 10240 | tf_op jit(solution)/shard_map/all_gather | solution.py:11
  88.3 0.6 copy-done.5
  88.9 0.7 slice-done.1
  89.6 0.7 slice-done.5
  90.3 0.7 slice-done.4
  91.2 10.0 %while.112 = (s32[]{:T(128)}, f32[4096]{0:T(1024)S(1)}, f32[4096]{0:T(1024)S(1)}, f32[512]{0:T(512)S(1)}, f32[512]{0:T(512)S(1)}, /*index=5*/f32[4096]{0:T(1024)...) while((s32[]{:T(128)}, f32[4096]{0:T(1024)S(1)}, ...), condition=%wide.region_21.22_spmd, body=%wide.region_18.0_spmd.sunk | while | flops 35912708 | bytes 2252979 | solution.py:76
  100.1 0.5 fusion.80
  101.2 1.8 all-gather.7
  103.0 1.8 all-gather.6
  104.9 12.0 %while.113 = (s32[]{:T(128)}, f32[64,4096]{1,0:T(8,128)S(1)}, f32[512]{0:T(512)S(1)}, f32[4096]{0:T(1024)S(1)}, f32[512]{0:T(512)S(1)}, /*index=5*/f32[4096]{0:T...) while((s32[]{:T(128)}, f32[64,4096]{1,0:T(8,128)S(1)}, ...), condition=%wide.region_23.24_spmd, body=%wide.region_22.23_spmd.sunk | while | flops 236748800 | bytes 2506939 | solution.py:93
  105.1 0.5 fusion.85
  105.6 0.8 fusion.86
  106.6 0.5 fusion.85
  107.1 0.8 fusion.86
  108.1 0.5 fusion.85
  108.6 0.8 fusion.86
  109.6 0.5 fusion.85
  110.1 0.8 fusion.86
  111.1 0.5 fusion.85
  111.6 0.8 fusion.86
  112.6 0.5 fusion.85
  113.1 0.8 fusion.86
  114.1 0.5 fusion.85
  114.6 0.8 fusion.86
  115.6 0.5 fusion.85
  116.1 0.8 fusion.86
  116.9 0.6 copy-done.6
  118.0 18.1 %all-reduce.3.cloned.1.call-done = f32[64,4096]{1,0:T(8,128)} async-done(((f32[64,4096]{1,0:T(8,128)}), f32[64,4096]{1,0:T(8,128)}) %all-reduce.3.cloned.1.call-update) | async-done | bytes 1048592 | tf_op jit(solution)/shard_map/psum | solution.py:94
  136.1 0.7 multiply_subtract_fusion.1
  136.8 56.0 %all-reduce.5.cloned.1.call-done = f32[64,4096]{1,0:T(8,128)} async-done(((f32[64,4096]{1,0:T(8,128)}), f32[64,4096]{1,0:T(8,128)}) %all-reduce.5.cloned.1.call-update) | async-done | bytes 1048592 | tf_op jit(solution)/shard_map/psum | solution.py:94
  192.8 2.3 %broadcast_multiply_fusion = f32[64,4096]{1,0:T(8,128)} fusion(f32[64,4096]{1,0:T(8,128)} %all-reduce.5.cloned.1.call-done), kind=kLoop, calls=%fused_computation.61 | loop fusion | flops 262144 | bytes 2097152 | tf_op jit(solution)/shard_map/div | solution.py:96
  (251 shorter events, 33.0 us)
Async XLA Ops:
  7.2 2.2 %copy-start.1 = (bf16[64,4096]{1,0:T(8,128)(2,1)S(1)}, bf16[64,4096]{1,0:T(8,128)(2,1)}, u32[]{:S(2)}) copy-start(bf16[64,4096]{1,0:T(8,128)(2,1)} %param.17) | copy-start | bytes 1572868
  7.2 128.9 %all-reduce.3.cloned.1.call-start = ((), (), s32[]{:S(2)}) async-start(), calls=%async_computation | async-start | bytes 2097152 | tf_op jit(solution)/shard_map/psum | solution.py:94
  8.2 1.2 copy-start.2
  29.3 0.6 copy-start.4
  41.8 0.7 slice-start.3
  42.5 0.7 slice-start.2
  75.8 0.6 copy-start.3
  88.3 0.6 copy-start.5
  88.9 0.7 slice-start.1
  89.6 0.7 slice-start.5
  90.3 0.7 slice-start.4
  90.3 0.7 slice-start
  116.9 0.6 copy-start.6
  116.9 1.0 copy-start
  117.9 74.9 %all-reduce.5.cloned.1.call-start = ((), (), s32[]{:S(2)}) async-start(), calls=%async_computation.1 | async-start | bytes 2097152 | tf_op jit(solution)/shard_map/psum | solution.py:94
Sparse Core Ops, SparseCore 0:
  118.0 17.9 all-reduce.2
  139.1 53.6 all-reduce.4
